TPU v7x, 128 devices: a whole 4x4x4 slice. The times are simulated.
128 devices in a mesh: group: 8 (over x_lo, z), tensor: 16 (over x_hi, y, core).
Axes of the slice: x: 4 (x_hi: 2, x_lo: 2; x = x_hi * 2 + x_lo), y: 4, z: 4, core: 2. Of those that a mesh axis runs over, the one named last changes fastest.
Arguments:
- hidden: bfloat16 [12288, 2048], P(('group', 'tensor')), may hold values from -20 to 20
- request_of: int32 [12288], P('group'), may hold values from 0 to 191, as said below
- positions: int32 [12288], P('group'), may hold values from 0 to 511, as said below
- page_table: int32 [8, 64], P('group'), may hold values from 0 to 63, each once within a row
- attn_gain: float32 [2048], replicated, may hold values from 0.5 to 1.5
- mlp_gain: float32 [2048], replicated, may hold values from 0.5 to 1.5
- wq: float32 [2048, 2048], P('group', 'tensor'), may hold values from -2 to 2
- wk: float32 [2048, 1024], P('group', 'tensor'), may hold values from -1 to 1
- wv: float32 [2048, 1024], P('group', 'tensor'), may hold values from -0.125 to 0.125
- wo: float32 [2048, 2048], P('tensor', 'group'), may hold values from -0.125 to 0.125
- w_gate: float32 [2048, 8192], P('group', 'tensor'), may hold values from -0.125 to 0.125
- w_up: float32 [2048, 8192], P('group', 'tensor'), may hold values from -0.125 to 0.125
- w_down: float32 [8192, 2048], P('tensor', 'group'), may hold values from -0.0625 to 0.0625
Outputs:
- layer_out: bfloat16 [12288, 2048], P(('group', 'tensor'))
- kv_pages: bfloat16 [512, 128, 2048], P('group', None, 'tensor')
Inputs may be any that keep to these rules, and one draw needn't show every extreme that they name: `request_of`: prompt numbers rise strictly along the token stream, starting at 0, and the last prompt of the stream has the number 12288 // 64 - 1; a prompt's rows are consecutive, and a prompt that reaches the last row of one block of 1536 rows continues at the first row of the next block. A prompt's rows have positions 0, 1, 2 and so on in order; a prompt has at most 512 rows, and one has exactly 512.
All inputs are finite; a program needn't handle non-finite values.
Results may differ from a plain program's by a relative error of at most 0.014.
Values may be sent and summed in bfloat16 or wider, within the bound.
A program may use at most 128 MiB of HBM per device.

v0:
```python
import jax
import jax.numpy as jnp
from jax import lax
from jax.sharding import PartitionSpec as P

QH = 16
KVH = 8
HD = 128
PAGE = 128
rope_base = 1000000.0
norm_eps = 1e-06


def partner(value, axis, distance):
    mask = 2**distance
    pairs = [(source, source ^ mask) for source in range(lax.axis_size(axis))]
    return lax.ppermute(value, axis, pairs)


def from_behind(block, axis, distance):
    devices = range(lax.axis_size(axis))
    route = [(i - distance, i) for i in devices if i - distance in devices]
    return lax.ppermute(block, axis, route)


def rms_scale(values, gain):
    square = jnp.mean(values * values, axis=-1, keepdims=True)
    return (values * lax.rsqrt(square + norm_eps) * gain).astype(jnp.bfloat16)


def rotate(values, places):
    half_dim = values.shape[-1] // 2
    frequency = rope_base ** (-(jnp.arange(half_dim, dtype=jnp.float32) * 2.0 / values.shape[-1]))
    angle = places.astype(jnp.float32)[:, None] * frequency[None, :]
    cosine = jnp.cos(angle)[:, None, :]
    sine = jnp.sin(angle)[:, None, :]
    widened = values.astype(jnp.float32)
    first = widened[..., :half_dim]
    second = widened[..., half_dim:]
    return jnp.concatenate(
        [first * cosine - second * sine, second * cosine + first * sine], axis=-1
    ).astype(jnp.bfloat16)


def join_halves(own_part, other_part):
    even = lax.axis_index("tensor") % 2 == 0
    lower = jnp.where(even, own_part, other_part)
    upper = jnp.where(even, other_part, own_part)
    return jnp.concatenate([lower, upper], axis=-1)


def contract_rows(acts, pieces):
    return tuple((jnp.dot(acts, piece, preferred_element_type=jnp.float32) for piece in pieces))


def body(
    hidden,
    request_of,
    positions,
    page_table,
    attn_gain,
    mlp_gain,
    wq,
    wk,
    wv,
    wo,
    w_gate,
    w_up,
    w_down,
):
    tensor_count = lax.axis_size("tensor")
    rows_dev = hidden.shape[0]
    tok_group = request_of.shape[0]
    query_heads = QH // tensor_count
    key_heads = max(1, KVH // tensor_count)
    group_ratio = QH // KVH
    residual = lax.all_gather(hidden, "tensor", axis=0, tiled=True).astype(jnp.float32)
    normed = rms_scale(residual, attn_gain)
    query_rows = wq.astype(jnp.bfloat16)
    key_rows = wk.astype(jnp.bfloat16)
    value_rows = wv.astype(jnp.bfloat16)
    other_key, other_value = partner((key_rows, value_rows), "tensor", 0)
    key_rows = join_halves(key_rows, other_key)
    value_rows = join_halves(value_rows, other_value)
    query_sum, key_sum, value_sum = contract_rows(
        normed,
        (
            lax.all_gather(query_rows, "group", axis=0, tiled=True),
            lax.all_gather(key_rows, "group", axis=0, tiled=True),
            lax.all_gather(value_rows, "group", axis=0, tiled=True),
        ),
    )
    query_raw = query_sum.astype(jnp.bfloat16)
    key_raw = key_sum.astype(jnp.bfloat16)
    value_raw = value_sum.astype(jnp.bfloat16)
    queries = rotate(query_raw.reshape(tok_group, query_heads, HD), positions)
    keys = rotate(key_raw.reshape(tok_group, key_heads, HD), positions)
    values = value_raw.reshape(tok_group, key_heads, HD)
    kv_rows = jnp.stack([keys, values], axis=2)
    earlier = from_behind(kv_rows, "group", 1)
    earlier_rows = earlier.shape[0]
    all_rows = jnp.concatenate([earlier, kv_rows], axis=0)
    all_keys = jnp.repeat(all_rows[:, :, 0], group_ratio, axis=1)[:, :query_heads]
    all_values = jnp.repeat(all_rows[:, :, 1], group_ratio, axis=1)[:, :query_heads]
    first_request = request_of[0]
    first_position = positions[0]
    same_local = (request_of[:, None] == request_of[None, :]) & (
        positions[None, :] <= positions[:, None]
    )
    same_earlier = (request_of[:, None] == first_request) & (
        jnp.arange(earlier_rows)[None, :] >= earlier_rows - first_position
    )
    visible = jnp.concatenate([same_earlier, same_local], axis=1)
    scores = jnp.einsum(
        "qhd,khd->hqk", queries, all_keys, preferred_element_type=jnp.float32
    ) * HD ** (-0.5)
    scores = jnp.where(visible[None], scores, -1e30)
    row_peak = jnp.max(scores, axis=-1, keepdims=True)
    probs = jnp.where(visible[None], jnp.exp(scores - row_peak), 0.0)
    total = jnp.sum(probs, axis=-1, keepdims=True)
    mixed_heads = jnp.einsum(
        "hqk,khd->qhd", probs.astype(jnp.bfloat16), all_values, preferred_element_type=jnp.float32
    ) / jnp.transpose(total, (1, 0, 2))
    attended = mixed_heads.astype(jnp.bfloat16).reshape(tok_group, query_heads * HD)
    out_rows = wo.astype(jnp.bfloat16)
    attn_part = jnp.dot(
        attended,
        lax.all_gather(out_rows, "group", axis=1, tiled=True),
        preferred_element_type=jnp.float32,
    )
    mixed = residual + lax.psum(attn_part.astype(jnp.bfloat16), "tensor").astype(jnp.float32)
    normed_mlp = rms_scale(mixed, mlp_gain)
    gate_rows = w_gate.astype(jnp.bfloat16)
    up_rows = w_up.astype(jnp.bfloat16)
    gate_sum, up_sum = contract_rows(
        normed_mlp,
        (
            lax.all_gather(gate_rows, "group", axis=0, tiled=True),
            lax.all_gather(up_rows, "group", axis=0, tiled=True),
        ),
    )
    activation = (jax.nn.silu(gate_sum) * up_sum).astype(jnp.bfloat16)
    down_rows = w_down.astype(jnp.bfloat16)
    down_part = jnp.dot(
        activation,
        lax.all_gather(down_rows, "group", axis=1, tiled=True),
        preferred_element_type=jnp.float32,
    )
    summed = lax.psum(down_part.astype(jnp.bfloat16), "tensor").astype(jnp.float32)
    first_row = lax.axis_index("tensor") * rows_dev
    own_mixed = lax.dynamic_slice_in_dim(mixed, first_row, rows_dev, 0)
    own_summed = lax.dynamic_slice_in_dim(summed, first_row, rows_dev, 0)
    layer_out = (own_mixed + own_summed).astype(jnp.bfloat16)
    pages = page_table.shape[1]
    changed = jnp.concatenate(
        [jnp.ones((1,), jnp.int32), (request_of[1:] != request_of[:-1]).astype(jnp.int32)]
    )
    opens = jnp.maximum(changed, (positions % PAGE == 0).astype(jnp.int32))
    logical = jnp.cumsum(opens) - 1
    chosen = jnp.sum(
        jnp.where(logical[:, None] == jnp.arange(pages)[None, :], page_table, 0), axis=1
    )
    target = chosen * PAGE + positions % PAGE
    width = 2 * KVH * HD // tensor_count
    flat_rows = kv_rows.reshape(tok_group, key_heads * 2 * HD)
    offset = lax.axis_index("tensor") * width % (key_heads * 2 * HD)
    own_slice = lax.dynamic_slice_in_dim(flat_rows, offset, width, 1)
    cache = jnp.zeros((pages * PAGE, width), jnp.bfloat16).at[target].set(own_slice)
    return (layer_out, cache.reshape(pages, PAGE, width))


def solution(mesh):
    placed = (
        P(("group", "tensor"), None),
        P("group"),
        P("group"),
        P("group", None),
        P(),
        P(),
        P("group", "tensor"),
        P("group", "tensor"),
        P("group", "tensor"),
        P("tensor", "group"),
        P("group", "tensor"),
        P("group", "tensor"),
        P("tensor", "group"),
    )
    return jax.shard_map(
        body,
        mesh=mesh,
        in_specs=placed,
        out_specs=(P(("group", "tensor"), None), P("group", None, "tensor")),
        check_vma=False,
    )
```

profile of v0, /device:TPU:0, one launch (start us, length us, event | category | flops | bytes accessed | tf_op | source)
XLA Modules:
  0.0 593.4 jit_solution(9900236413319749413)
XLA Ops:
  8.0 0.0 copy-start.8
  8.0 0.0 all-gather.5.cloned.1.call-start
  8.1 0.7 all-gather.5.cloned.1.call-update
  8.8 0.0 all-reduce.3.cloned.1.call-start
  8.8 0.8 convert_element_type.103
  9.6 0.8 convert_element_type.108
  10.5 0.5 collective-permute-start.1
  11.0 0.9 convert_element_type.110
  11.9 1.2 slice.43
  13.1 1.2 slice.42
  14.3 0.8 slice_compare_fusion
  15.2 0.8 maximum_bitcast_fusion
  15.9 0.3 reduce-window.9
  16.2 0.1 slice.57
  16.3 0.9 convert_element_type.117
  17.9 0.1 slice_reduce_fusion
  18.0 0.1 add_bitcast_fusion
  18.1 0.8 select_reduce_fusion
  18.9 1.4 iota_compare_fusion.1
  20.2 0.8 compare_select_fusion
  21.0 30.5 %all_gather.27 = bf16[2048,128]{1,0:T(8,128)(2,1)S(1)} all-gather(bf16[256,128]{1,0:T(8,128)(2,1)S(1)} %convert_element_type.110), channel_id=1, replica_groups=mesh['group'=8,'tensor'=16] {'group'}, dimensions={0}, use_global_device_ids=true | all-gather | bytes 589824 | tf_op jit(solution)/shard_map/all_gather | solution.py:88
  51.6 32.5 %all_gather.28 = bf16[128,2048]{1,0:T(8,128)(2,1)} all-gather(bf16[128,256]{1,0:T(8,128)(2,1)S(1)} %convert_element_type.117), channel_id=1, replica_groups=mesh['group'=8,'tensor'=16] {'group'}, dimensions={1}, use_global_device_ids=true | all-gather | bytes 589824 | tf_op jit(solution)/shard_map/all_gather | solution.py:128
  84.0 3.3 compare_and_fusion
  87.5 29.4 %all_gather.25 = bf16[2048,128]{0,1:T(8,128)(2,1)S(1)} all-gather(bf16[256,128]{0,1:T(8,128)(2,1)S(1)} %pad_maximum_fusion.1), channel_id=1, replica_groups=mesh['group'=8,'tensor'=16] {'group'}, dimensions={0}, use_global_device_ids=true | all-gather | bytes 589824 | tf_op jit(solution)/shard_map/all_gather | solution.py:89
  116.8 30.9 %all_gather.26 = bf16[2048,128]{0,1:T(8,128)(2,1)} all-gather(bf16[256,128]{0,1:T(8,128)(2,1)S(1)} %pad_maximum_fusion.2), channel_id=1, replica_groups=mesh['group'=8,'tensor'=16] {'group'}, dimensions={0}, use_global_device_ids=true | all-gather | bytes 589824 | tf_op jit(solution)/shard_map/all_gather | solution.py:90
  147.7 4.2 fusion.1
  152.0 0.3 copy-done
  152.3 1.5 fusion.3
  153.8 2.2 fusion.13
  156.0 2.2 fusion.16
  158.3 2.2 fusion.14
  160.5 1.7 fusion.52
  162.2 0.1 pad_maximum_fusion
  162.3 4.2 collective-permute-start.2
  166.5 1.5 broadcast_and_fusion
  168.1 7.7 %collective-permute-done.2 = bf16[1536,1,2,128]{0,3,2,1:T(8,128)(2,1)S(1)} collective-permute-done((bf16[1536,1,2,128]{0,3,2,1:T(8,128)(2,1)S(1)}, bf16[1536,1,2,128]{0,3,2,1:T(8,128)(2,1)S(1)}, u32[]{:S(2)}, u32[]{:S(2)}) %collective-permute-start.2) | collective-permute-done | bytes 786464 | tf_op jit(solution)/shard_map/ppermute | solution.py:23
  175.8 0.2 maximum_maximum_fusion
  176.0 0.0 copy-start.3
  176.0 4.1 fusion
  180.1 6.4 %copy-done.1 = f32[1536,3072]{1,0:T(8,128)} copy-done((f32[1536,3072]{1,0:T(8,128)}, f32[1536,3072]{1,0:T(8,128)S(1)}, u32[]{:S(2)}) %copy-start.1) | copy-done | bytes 18874392
  186.5 6.4 %fusion.4 = f32[1536]{0:T(1024)S(1)} fusion(f32[1536,3072]{1,0:T(8,128)S(1)} %get-tuple-element.17, f32[1536]{0:T(1024)S(1)} %get-tuple-element.16, pred[1536,1536]{1,0:T(32,128)(4,1)S(1)} %compare_and_fusion, pred[1536,1536]{1,0:T(32,128)(4,1)S(1)} %broadcast_and_fusion), kind=kLoop, calls=%fused_computation.13 | loop fusion | flops 28310016 | bytes 23605248 | tf_op jit(solution)/shard_map/reduce_sum | solution.py:120
  192.9 14.1 %convolution_convert_fusion.1 = bf16[1536,2048]{1,0:T(8,128)(2,1)} fusion(bf16[128,2048]{1,0:T(8,128)(2,1)} %all_gather.28, f32[1536,3072]{1,0:T(8,128)} %copy-done.1, f32[1536]{0:T(1024)S(1)} %get-tuple-element.16, bf16[3072,1,2,128]{0,3,2,1:T(8,128)(2,1)} %copy-done.3, f32[1536]{0:T(1024)S(1)} %fusion.4, pred[1536,1536]{1,0:T(32,128)(4,1)S(1)} %compare_and_fusion, ...), kind=kOutput, calls=%fused_computation.18 | convolution fusion | flops 2045116416 | bytes 31207424 | tf_op jit(solution)/shard_map/dot_general | solution.py:126
  207.0 0.0 all-reduce.3.cloned.1.call-update
  207.1 0.0 all-gather.7.cloned.1.call-start
  207.1 1.0 copy-done.4
  208.1 0.8 convert_element_type.121
  208.8 0.0 all-gather.7.cloned.1.call-update
  208.8 0.0 all-gather.11.cloned.1.call-start
  208.9 0.7 convert_element_type.124
  209.6 0.0 all-gather.11.cloned.1.call-update
  209.7 0.0 all-gather.9.cloned.1.call-start
  209.7 0.7 convert_element_type.122
  210.5 0.0 all-gather.9.cloned.1.call-update
  210.5 0.0 copy-start.11
  210.5 0.3 all-reduce.5.cloned.1.call-start
  210.8 179.3 %all-reduce.3.cloned.1.call-done = bf16[1536,2048]{1,0:T(8,128)(2,1)} async-done(((bf16[1536,2048]{1,0:T(8,128)(2,1)}), bf16[1536,2048]{1,0:T(8,128)(2,1)}) %all-reduce.3.cloned.1.call-update) | async-done | bytes 6291472 | tf_op jit(solution)/shard_map/psum | solution.py:131
  390.1 11.2 %multiply_reduce_fusion = (f32[1536]{0:T(1024)S(1)}, f32[1536,2048]{1,0:T(8,128)}) fusion(bf16[1536,2048]{1,0:T(8,128)(2,1)} %all-reduce.3.cloned.1.call-done, bf16[1536,2048]{1,0:T(8,128)(2,1)} %all-gather.5.cloned.1.call-done), kind=kLoop, calls=%fused_computation.12 | loop fusion | flops 15727104 | bytes 25171968 | tf_op jit(solution)/shard_map/reduce_sum | solution.py:27
  401.3 10.4 %fusion.64 = f32[1536,512]{1,0:T(8,128)} fusion(bf16[2048,512]{1,0:T(8,128)(2,1)} %all-gather.7.cloned.1.call-done, f32[2048]{0:T(1024)S(1)} %copy-done.11, f32[1536]{0:T(1024)S(1)} %add_rsqrt_fusion, bf16[1536,2048]{1,0:T(8,128)(2,1)} %all-gather.5.cloned.1.call-done, bf16[1536,2048]{1,0:T(8,128)(2,1)} %all-reduce.3.cloned.1.call-done), kind=kOutput, calls=%fused_computation.96 | convolution fusion | flops 3240099840 | bytes 17840128 | tf_op jit(solution)/shard_map/dot_general | solution.py:53
  411.7 15.3 %convolution_convert_fusion = bf16[1536,2048]{1,0:T(8,128)(2,1)} fusion(bf16[512,2048]{1,0:T(8,128)(2,1)} %all-gather.11.cloned.1.call-done, bf16[2048,512]{1,0:T(8,128)(2,1)} %all-gather.9.cloned.1.call-done, f32[1536,512]{1,0:T(8,128)} %fusion.64, f32[2048]{0:T(1024)S(1)} %copy-done.11, f32[1536]{0:T(1024)S(1)} %add_rsqrt_fusion, ...), kind=kOutput, calls=%fused_computation.17 | convolution fusion | flops 6469189632 | bytes 26228736 | tf_op jit(solution)/shard_map/dot_general | solution.py:144
  427.0 0.0 all-reduce.5.cloned.1.call-update
  427.1 0.2 copy.17
  427.3 6.1 %scatter_custom_fusion = bf16[8192,128]{1,0:T(8,128)(2,1)} fusion(s32[1536]{0:T(1024)S(1)} %get-tuple-element.14, bf16[1536,128]{1,0:T(8,128)(2,1)S(1)} %copy.17, bf16[]{:T(256)} %constant.84.clone.1), kind=kCustom, calls=%fused_computation.35 | custom fusion | bytes 2097154 | tf_op jit(solution)/shard_map/scatter | solution.py:168
  433.4 150.6 %all-reduce.5.cloned.1.call-done = bf16[1536,2048]{1,0:T(8,128)(2,1)} async-done(((bf16[1536,2048]{1,0:T(8,128)(2,1)}), bf16[1536,2048]{1,0:T(8,128)(2,1)}) %all-reduce.5.cloned.1.call-update) | async-done | bytes 6291472 | tf_op jit(solution)/shard_map/psum | solution.py:149
  584.0 2.1 add_convert_fusion
  (33 shorter events, 0.2 us)
Async XLA Ops:
  8.0 79.4 %copy-start.9 = (f32[256,64]{0,1:T(8,128)S(1)}, f32[256,64]{0,1:T(8,128)}, u32[]{:S(2)}) copy-start(f32[256,64]{0,1:T(8,128)} %param.20) | copy-start | bytes 196612
  8.0 79.4 %copy-start.8 = (f32[256,64]{0,1:T(8,128)S(1)}, f32[256,64]{0,1:T(8,128)}, u32[]{:S(2)}) copy-start(f32[256,64]{0,1:T(8,128)} %param.21) | copy-start | bytes 196612
  8.0 139.7 %all-gather.5.cloned.1.call-start = ((), (), s32[]{:S(2)}) async-start(), calls=%async_computation | async-start | bytes 6684672 | tf_op jit(solution)/shard_map/all_gather | solution.py:77
  8.8 381.3 %all-reduce.3.cloned.1.call-start = ((), (), s32[]{:S(2)}) async-start(), calls=%async_computation.1 | async-start | bytes 12582912 | tf_op jit(solution)/shard_map/psum | solution.py:131
  9.6 77.7 %collective-permute-start = (bf16[256,64]{0,1:T(8,128)(2,1)S(1)}, bf16[256,64]{0,1:T(8,128)(2,1)S(1)}, u32[]{:S(2)}, u32[]{:S(2)}) collective-permute-start(bf16[256,64]{0,1:T(8,128)(2,1)S(1)} %convert_element_type.103), channel_id=1, source_target_pairs={{0,1},{1,0},{2,3},{3,2},{4,5},{5,4},{6,7},{7,6},{8,9},{9,8},{10,11... | collective-permute-start | bytes 98312 | tf_op jit(solution)/shard_map/ppermute | solution.py:17
  10.5 76.9 %collective-permute-start.1 = (bf16[256,64]{0,1:T(8,128)(2,1)S(1)}, bf16[256,64]{0,1:T(8,128)(2,1)S(1)}, u32[]{:S(2)}, u32[]{:S(2)}) collective-permute-start(bf16[256,64]{0,1:T(8,128)(2,1)S(1)} %convert_element_type.108), channel_id=1, source_target_pairs={{0,1},{1,0},{2,3},{3,2},{4,5},{5,4},{6,7},{7,6},{8,9},{9,8},{10,11... | collective-permute-start | bytes 98312 | tf_op jit(solution)/shard_map/ppermute | solution.py:17
  84.0 67.9 %copy-start.10 = (f32[2048]{0:T(1024)S(1)}, f32[2048]{0:T(1024)}, u32[]{:S(2)}) copy-start(f32[2048]{0:T(1024)} %param.17) | copy-start | bytes 24580
  147.7 4.6 copy-start
  156.0 2.2 copy-start.7
  162.3 13.5 %collective-permute-start.2 = (bf16[1536,1,2,128]{0,3,2,1:T(8,128)(2,1)S(1)}, bf16[1536,1,2,128]{0,3,2,1:T(8,128)(2,1)S(1)}, u32[]{:S(2)}, u32[]{:S(2)}) collective-permute-start(bf16[1536,1,2,128]{0,3,2,1:T(8,128)(2,1)S(1)} %pad_maximum_fusion), channel_id=1, source_target_pairs={{0,16},{16,32},{32,48},{48,64},{64,80},{80,96},{96,112},{1,17},{17... | collective-permute-start | bytes 2359304 | tf_op jit(solution)/shard_map/ppermute | solution.py:23
  168.1 12.0 %copy-start.2 = (pred[1536,1536]{1,0:T(32,128)(4,1)}, pred[1536,1536]{1,0:T(32,128)(4,1)S(1)}, u32[]{:S(2)}) copy-start(pred[1536,1536]{1,0:T(32,128)(4,1)S(1)} %broadcast_and_fusion) | copy-start | bytes 7077892
  176.0 4.1 copy-start.3
  180.1 6.5 %copy-start.1 = (f32[1536,3072]{1,0:T(8,128)}, f32[1536,3072]{1,0:T(8,128)S(1)}, u32[]{:S(2)}) copy-start(f32[1536,3072]{1,0:T(8,128)S(1)} %get-tuple-element.17) | copy-start | bytes 56623108
  207.0 1.0 copy-start.4
  207.0 1.9 copy-start.5
  207.0 2.7 copy-start.6
  207.1 194.2 %all-gather.7.cloned.1.call-start = ((), (), s32[]{:S(2)}) async-start(), calls=%async_computation.2 | async-start | bytes 2359296 | tf_op jit(solution)/shard_map/all_gather | solution.py:138
  208.8 202.8 %all-gather.11.cloned.1.call-start = ((), (), s32[]{:S(2)}) async-start(), calls=%async_computation.4 | async-start | bytes 2359296 | tf_op jit(solution)/shard_map/all_gather | solution.py:146
  209.7 202.0 %all-gather.9.cloned.1.call-start = ((), (), s32[]{:S(2)}) async-start(), calls=%async_computation.3 | async-start | bytes 2359296 | tf_op jit(solution)/shard_map/all_gather | solution.py:139
  210.5 190.8 %copy-start.11 = (f32[2048]{0:T(1024)S(1)}, f32[2048]{0:T(1024)}, u32[]{:S(2)}) copy-start(f32[2048]{0:T(1024)} %param.18) | copy-start | bytes 24580
  210.5 373.5 %all-reduce.5.cloned.1.call-start = ((), (), s32[]{:S(2)}) async-start(), calls=%async_computation.5 | async-start | bytes 12582912 | tf_op jit(solution)/shard_map/psum | solution.py:149
Sparse Core Ops, SparseCore 0:
  11.3 70.2 all-gather.4
  207.2 182.8 all-reduce.2
  427.1 156.8 all-reduce.4
Sparse Core Ops, SparseCore 1:
  209.2 49.1 all-gather.6
  260.3 41.6 all-gather.10
  304.1 50.6 all-gather.8
where the time goes:
time: 594 us; the launch traced here: 593 us
  waiting for transfers between devices  338 us (57%)
  blocking collectives  123 us (21%)
  matrix products  50.5 us (9%)
  other arithmetic  42.9 us (7%)
  local copies, waits for them, and re-layouts  16.7 us (3%)
  between operations  16.4 us (3%)
    psum x1, waiting for transfers between devices, body(): lax.psum(attn_part.astype(jnp.bfloat16), 'tensor').astype(jnp.float32)  179 us
    psum x1, waiting for transfers between devices, body(): lax.psum(down_part.astype(jnp.bfloat16), 'tensor').astype(jnp.float32)  151 us
    all_gather x1, blocking collectives, body(): lax.all_gather(out_rows, 'group', axis=1, tiled=True)  32.5 us
    all_gather x1, blocking collectives, body(): lax.all_gather(value_rows, 'group', axis=0, tiled=True)  30.9 us
    all_gather x1, blocking collectives, body(): lax.all_gather(query_rows, 'group', axis=0, tiled=True)  30.5 us
    all_gather x1, blocking collectives, body(): lax.all_gather(key_rows, 'group', axis=0, tiled=True)  29.4 us
    dot_general x4, matrix products, contract_rows(): jnp.dot(acts, piece, preferred_element_type=jnp.float32)  17 us
    reduce_sum x2, other arithmetic, rms_scale(): square = jnp.mean(values * values, axis=-1, keepdims=True)  15.4 us
  transfers between devices with their start and end apart: 9, of which 3 were waited for; matrix products, arithmetic and copies ran while one was open for 8% of the time, Pallas kernels for 0%

commit v1 on v0

--- a/solution.py
+++ b/solution.py
@@ -9,6 +9,11 @@
 PAGE = 128
 rope_base = 1000000.0
 norm_eps = 1e-06
+
+
+def gather_over(x, name, dim):
+    sent = jnp.stack([x] * lax.axis_size(name))
+    return jnp.concatenate(lax.all_to_all(sent, name, 0, 0), axis=dim)
 
 
 def partner(value, axis, distance):
@@ -86,7 +91,7 @@
         normed,
         (
             lax.all_gather(query_rows, "group", axis=0, tiled=True),
-            lax.all_gather(key_rows, "group", axis=0, tiled=True),
+            gather_over(key_rows, "group", 0),
             lax.all_gather(value_rows, "group", axis=0, tiled=True),
         ),
     )

time: 594 us -> 578 us (0.973)
  blocking collectives: 123 us -> 96.5 us
    all_gather x1 -> x0, blocking collectives: 29.4 us -> none  [body(): lax.all_gather(key_rows, 'group', axis=0, tiled=True)]
  transfers between devices with their start and end apart: 9 -> 10, of which waited for: 3 -> 3; matrix products, arithmetic and copies ran while one was open for 8% -> 10% of each run, Pallas kernels for 0% -> 0%
where the time goes in v1:
time: 578 us
  waiting for transfers between devices  340 us (59%)
  blocking collectives  96.5 us (17%)
  matrix products  53.5 us (9%)
  other arithmetic  45.5 us (8%)
  local copies, waits for them, and re-layouts  17.7 us (3%)
  between operations  16.4 us (3%)
  starting transfers between devices  8.22 us (1%)
    psum x1, waiting for transfers between devices, body(): lax.psum(attn_part.astype(jnp.bfloat16), 'tensor').astype(jnp.float32)  181 us
    psum x1, waiting for transfers between devices, body(): lax.psum(down_part.astype(jnp.bfloat16), 'tensor').astype(jnp.float32)  151 us
    all_gather x1, blocking collectives, body(): lax.all_gather(value_rows, 'group', axis=0, tiled=True)  33.5 us
    all_gather x1, blocking collectives, body(): lax.all_gather(out_rows, 'group', axis=1, tiled=True)  32.5 us
    all_gather x1, blocking collectives, body(): lax.all_gather(query_rows, 'group', axis=0, tiled=True)  30.5 us
    dot_general x4, matrix products, contract_rows(): jnp.dot(acts, piece, preferred_element_type=jnp.float32)  20 us
    reduce_sum x2, other arithmetic, rms_scale(): square = jnp.mean(values * values, axis=-1, keepdims=True)  15.4 us
    dot_general x1, matrix products, body(): jnp.dot(activation, lax.all_gather(down_rows, 'group', axis=1, tiled=True...  15.4 us
  transfers between devices with their start and end apart: 10, of which 3 were waited for; matrix products, arithmetic and copies ran while one was open for 10% of the time, Pallas kernels for 0%

profile of v1, /device:TPU:0, one launch (start us, length us, event | category | flops | bytes accessed | tf_op | source)
XLA Modules:
  0.0 577.7 jit_solution(3232758222370022637)
XLA Ops:
  8.0 0.0 copy-start.9
  8.0 0.0 all-gather.5.cloned.1.call-start
  8.1 0.7 all-gather.5.cloned.1.call-update
  8.8 0.8 convert_element_type.103
  9.6 0.8 convert_element_type.108
  10.4 0.5 collective-permute-start.1
  11.0 0.9 convert_element_type.110
  11.9 1.2 slice.43
  13.1 1.2 slice.42
  14.3 0.8 slice_compare_fusion
  15.1 0.8 maximum_bitcast_fusion
  15.9 0.3 reduce-window.9
  16.2 0.1 slice.57
  16.3 0.9 convert_element_type.117
  17.8 0.1 slice_reduce_fusion
  18.0 0.1 add_bitcast_fusion
  18.0 0.8 select_reduce_fusion
  18.8 1.4 iota_compare_fusion.1
  20.2 0.8 compare_select_fusion
  21.0 30.5 %all_gather.23 = bf16[2048,128]{1,0:T(8,128)(2,1)S(1)} all-gather(bf16[256,128]{1,0:T(8,128)(2,1)S(1)} %convert_element_type.110), channel_id=1, replica_groups=mesh['group'=8,'tensor'=16] {'group'}, dimensions={0}, use_global_device_ids=true | all-gather | bytes 589824 | tf_op jit(solution)/shard_map/all_gather | solution.py:93
  51.4 32.5 %all_gather.24 = bf16[128,2048]{1,0:T(8,128)(2,1)} all-gather(bf16[128,256]{1,0:T(8,128)(2,1)S(1)} %convert_element_type.117), channel_id=1, replica_groups=mesh['group'=8,'tensor'=16] {'group'}, dimensions={1}, use_global_device_ids=true | all-gather | bytes 589824 | tf_op jit(solution)/shard_map/all_gather | solution.py:133
  84.0 3.3 compare_and_fusion
  87.4 0.1 copy.18
  87.5 0.9 stack.4
  88.4 5.6 all-to-all-start
  94.0 0.0 all-reduce.3.cloned.1.call-start
  94.1 33.5 %all_gather.22 = bf16[2048,128]{0,1:T(8,128)(2,1)} all-gather(bf16[256,128]{0,1:T(8,128)(2,1)S(1)} %pad_maximum_fusion.2), channel_id=1, replica_groups=mesh['group'=8,'tensor'=16] {'group'}, dimensions={0}, use_global_device_ids=true | all-gather | bytes 589824 | tf_op jit(solution)/shard_map/all_gather | solution.py:95
  127.5 4.2 fusion.1
  131.8 0.3 copy-done.1
  132.1 4.1 fusion.3
  136.2 5.2 fusion.13
  141.4 2.2 fusion.16
  143.7 2.2 fusion.14
  145.9 1.7 fusion.52
  147.6 0.1 pad_maximum_fusion
  147.7 1.6 collective-permute-start.2
  149.3 1.5 broadcast_and_fusion
  150.9 7.7 %collective-permute-done.2 = bf16[1536,1,2,128]{0,3,2,1:T(8,128)(2,1)S(1)} collective-permute-done((bf16[1536,1,2,128]{0,3,2,1:T(8,128)(2,1)S(1)}, bf16[1536,1,2,128]{0,3,2,1:T(8,128)(2,1)S(1)}, u32[]{:S(2)}, u32[]{:S(2)}) %collective-permute-start.2) | collective-permute-done | bytes 786464 | tf_op jit(solution)/shard_map/ppermute | solution.py:28
  158.6 0.2 maximum_maximum_fusion
  158.8 4.1 fusion
  162.9 6.4 %copy-done.2 = f32[1536,3072]{1,0:T(8,128)} copy-done((f32[1536,3072]{1,0:T(8,128)}, f32[1536,3072]{1,0:T(8,128)S(1)}, u32[]{:S(2)}) %copy-start.2) | copy-done | bytes 18874392
  169.3 6.4 %fusion.4 = f32[1536]{0:T(1024)S(1)} fusion(f32[1536,3072]{1,0:T(8,128)S(1)} %get-tuple-element.17, f32[1536]{0:T(1024)S(1)} %get-tuple-element.16, pred[1536,1536]{1,0:T(32,128)(4,1)S(1)} %compare_and_fusion, pred[1536,1536]{1,0:T(32,128)(4,1)S(1)} %broadcast_and_fusion), kind=kLoop, calls=%fused_computation.13 | loop fusion | flops 28310016 | bytes 23605248 | tf_op jit(solution)/shard_map/reduce_sum | solution.py:125
  175.7 14.1 %convolution_convert_fusion.1 = bf16[1536,2048]{1,0:T(8,128)(2,1)} fusion(bf16[128,2048]{1,0:T(8,128)(2,1)} %all_gather.24, f32[1536,3072]{1,0:T(8,128)} %copy-done.2, f32[1536]{0:T(1024)S(1)} %get-tuple-element.16, bf16[3072,1,2,128]{0,3,2,1:T(8,128)(2,1)} %copy-done.4, f32[1536]{0:T(1024)S(1)} %fusion.4, pred[1536,1536]{1,0:T(32,128)(4,1)S(1)} %compare_and_fusion, ...), kind=kOutput, calls=%fused_computation.18 | convolution fusion | flops 2045116416 | bytes 31207424 | tf_op jit(solution)/shard_map/dot_general | solution.py:131
  189.8 0.0 all-reduce.3.cloned.1.call-update
  189.9 0.0 all-gather.7.cloned.1.call-start
  189.9 1.0 copy-done.5
  190.9 0.7 convert_element_type.121
  191.6 0.0 all-gather.7.cloned.1.call-update
  191.6 0.0 all-gather.11.cloned.1.call-start
  191.7 0.7 convert_element_type.124
  192.4 0.0 all-gather.11.cloned.1.call-update
  192.4 0.0 all-gather.9.cloned.1.call-start
  192.5 0.7 convert_element_type.122
  193.2 0.0 all-gather.9.cloned.1.call-update
  193.3 0.3 all-reduce.5.cloned.1.call-start
  193.5 180.5 %all-reduce.3.cloned.1.call-done = bf16[1536,2048]{1,0:T(8,128)(2,1)} async-done(((bf16[1536,2048]{1,0:T(8,128)(2,1)}), bf16[1536,2048]{1,0:T(8,128)(2,1)}) %all-reduce.3.cloned.1.call-update) | async-done | bytes 6291472 | tf_op jit(solution)/shard_map/psum | solution.py:136
  374.1 11.2 %multiply_reduce_fusion = (f32[1536]{0:T(1024)S(1)}, f32[1536,2048]{1,0:T(8,128)}) fusion(bf16[1536,2048]{1,0:T(8,128)(2,1)} %all-reduce.3.cloned.1.call-done, bf16[1536,2048]{1,0:T(8,128)(2,1)} %all-gather.5.cloned.1.call-done), kind=kLoop, calls=%fused_computation.12 | loop fusion | flops 15727104 | bytes 25171968 | tf_op jit(solution)/shard_map/reduce_sum | solution.py:32
  385.3 10.4 %fusion.64 = f32[1536,512]{1,0:T(8,128)} fusion(bf16[2048,512]{1,0:T(8,128)(2,1)} %all-gather.7.cloned.1.call-done, f32[2048]{0:T(1024)S(1)} %copy-done.12, f32[1536]{0:T(1024)S(1)} %add_rsqrt_fusion, bf16[1536,2048]{1,0:T(8,128)(2,1)} %all-gather.5.cloned.1.call-done, bf16[1536,2048]{1,0:T(8,128)(2,1)} %all-reduce.3.cloned.1.call-done), kind=kOutput, calls=%fused_computation.96 | convolution fusion | flops 3240099840 | bytes 17840128 | tf_op jit(solution)/shard_map/dot_general | solution.py:58
  395.7 15.4 %convolution_convert_fusion = bf16[1536,2048]{1,0:T(8,128)(2,1)} fusion(bf16[512,2048]{1,0:T(8,128)(2,1)} %all-gather.11.cloned.1.call-done, bf16[2048,512]{1,0:T(8,128)(2,1)} %all-gather.9.cloned.1.call-done, f32[1536,512]{1,0:T(8,128)} %fusion.64, f32[2048]{0:T(1024)S(1)} %copy-done.12, f32[1536]{0:T(1024)S(1)} %add_rsqrt_fusion, ...), kind=kOutput, calls=%fused_computation.17 | convolution fusion | flops 6469189632 | bytes 26228736 | tf_op jit(solution)/shard_map/dot_general | solution.py:149
  411.0 0.0 all-reduce.5.cloned.1.call-update
  411.1 0.2 copy.20
  411.4 6.1 %scatter_custom_fusion = bf16[8192,128]{1,0:T(8,128)(2,1)} fusion(s32[1536]{0:T(1024)S(1)} %get-tuple-element.14, bf16[1536,128]{1,0:T(8,128)(2,1)S(1)} %copy.20, bf16[]{:T(256)} %constant.84.clone.1), kind=kCustom, calls=%fused_computation.35 | custom fusion | bytes 2097154 | tf_op jit(solution)/shard_map/scatter | solution.py:173
  417.5 150.8 %all-reduce.5.cloned.1.call-done = bf16[1536,2048]{1,0:T(8,128)(2,1)} async-done(((bf16[1536,2048]{1,0:T(8,128)(2,1)}), bf16[1536,2048]{1,0:T(8,128)(2,1)}) %all-reduce.5.cloned.1.call-update) | async-done | bytes 6291472 | tf_op jit(solution)/shard_map/psum | solution.py:154
  568.3 2.1 add_convert_fusion
  (38 shorter events, 0.2 us)
Async XLA Ops:
  8.0 79.3 %copy-start.10 = (f32[256,64]{0,1:T(8,128)S(1)}, f32[256,64]{0,1:T(8,128)}, u32[]{:S(2)}) copy-start(f32[256,64]{0,1:T(8,128)} %param.20) | copy-start | bytes 196612
  8.0 79.3 %copy-start.9 = (f32[256,64]{0,1:T(8,128)S(1)}, f32[256,64]{0,1:T(8,128)}, u32[]{:S(2)}) copy-start(f32[256,64]{0,1:T(8,128)} %param.21) | copy-start | bytes 196612
  8.0 119.5 %all-gather.5.cloned.1.call-start = ((), (), s32[]{:S(2)}) async-start(), calls=%async_computation.1 | async-start | bytes 6684672 | tf_op jit(solution)/shard_map/all_gather | solution.py:82
  9.6 77.7 %collective-permute-start = (bf16[256,64]{0,1:T(8,128)(2,1)S(1)}, bf16[256,64]{0,1:T(8,128)(2,1)S(1)}, u32[]{:S(2)}, u32[]{:S(2)}) collective-permute-start(bf16[256,64]{0,1:T(8,128)(2,1)S(1)} %convert_element_type.103), channel_id=1, source_target_pairs={{0,1},{1,0},{2,3},{3,2},{4,5},{5,4},{6,7},{7,6},{8,9},{9,8},{10,11... | collective-permute-start | bytes 98312 | tf_op jit(solution)/shard_map/ppermute | solution.py:22
  10.4 76.9 %collective-permute-start.1 = (bf16[256,64]{0,1:T(8,128)(2,1)S(1)}, bf16[256,64]{0,1:T(8,128)(2,1)S(1)}, u32[]{:S(2)}, u32[]{:S(2)}) collective-permute-start(bf16[256,64]{0,1:T(8,128)(2,1)S(1)} %convert_element_type.108), channel_id=1, source_target_pairs={{0,1},{1,0},{2,3},{3,2},{4,5},{5,4},{6,7},{7,6},{8,9},{9,8},{10,11... | collective-permute-start | bytes 98312 | tf_op jit(solution)/shard_map/ppermute | solution.py:22
  87.3 44.5 %copy-start.11 = (f32[2048]{0:T(1024)S(1)}, f32[2048]{0:T(1024)}, u32[]{:S(2)}) copy-start(f32[2048]{0:T(1024)} %param.17) | copy-start | bytes 24580
  88.4 47.9 %all-to-all-start = ((bf16[8,256,128]{2,1,0:T(8,128)(2,1)}), bf16[8,256,128]{2,1,0:T(8,128)(2,1)S(1)}, u32[]{:S(2)}, u32[]{:S(2)}) async-start(bf16[8,256,128]{2,1,0:T(8,128)(2,1)} %stack.4), calls=%async_computation | async-start | bytes 1048576 | tf_op jit(solution)/shard_map/all_to_all | solution.py:16
  94.0 280.1 %all-reduce.3.cloned.1.call-start = ((), (), s32[]{:S(2)}) async-start(), calls=%async_computation.2 | async-start | bytes 12582912 | tf_op jit(solution)/shard_map/psum | solution.py:136
  127.5 4.6 copy-start.1
  136.2 5.2 copy-start
  141.4 2.2 copy-start.8
  147.7 10.9 %collective-permute-start.2 = (bf16[1536,1,2,128]{0,3,2,1:T(8,128)(2,1)S(1)}, bf16[1536,1,2,128]{0,3,2,1:T(8,128)(2,1)S(1)}, u32[]{:S(2)}, u32[]{:S(2)}) collective-permute-start(bf16[1536,1,2,128]{0,3,2,1:T(8,128)(2,1)S(1)} %pad_maximum_fusion), channel_id=1, source_target_pairs={{0,16},{16,32},{32,48},{48,64},{64,80},{80,96},{96,112},{1,17},{17... | collective-permute-start | bytes 2359304 | tf_op jit(solution)/shard_map/ppermute | solution.py:28
  150.9 12.0 %copy-start.3 = (pred[1536,1536]{1,0:T(32,128)(4,1)}, pred[1536,1536]{1,0:T(32,128)(4,1)S(1)}, u32[]{:S(2)}) copy-start(pred[1536,1536]{1,0:T(32,128)(4,1)S(1)} %broadcast_and_fusion) | copy-start | bytes 7077892
  158.8 4.1 copy-start.4
  162.9 6.5 %copy-start.2 = (f32[1536,3072]{1,0:T(8,128)}, f32[1536,3072]{1,0:T(8,128)S(1)}, u32[]{:S(2)}) copy-start(f32[1536,3072]{1,0:T(8,128)S(1)} %get-tuple-element.17) | copy-start | bytes 56623108
  189.8 1.0 copy-start.5
  189.8 1.9 copy-start.6
  189.8 2.7 copy-start.7
  189.9 195.4 %all-gather.7.cloned.1.call-start = ((), (), s32[]{:S(2)}) async-start(), calls=%async_computation.3 | async-start | bytes 2359296 | tf_op jit(solution)/shard_map/all_gather | solution.py:143
  191.6 204.1 %all-gather.11.cloned.1.call-start = ((), (), s32[]{:S(2)}) async-start(), calls=%async_computation.5 | async-start | bytes 2359296 | tf_op jit(solution)/shard_map/all_gather | solution.py:151
  192.4 203.3 %all-gather.9.cloned.1.call-start = ((), (), s32[]{:S(2)}) async-start(), calls=%async_computation.4 | async-start | bytes 2359296 | tf_op jit(solution)/shard_map/all_gather | solution.py:144
  193.3 192.0 %copy-start.12 = (f32[2048]{0:T(1024)S(1)}, f32[2048]{0:T(1024)}, u32[]{:S(2)}) copy-start(f32[2048]{0:T(1024)} %param.18) | copy-start | bytes 24580
  193.3 375.1 %all-reduce.5.cloned.1.call-start = ((), (), s32[]{:S(2)}) async-start(), calls=%async_computation.6 | async-start | bytes 12582912 | tf_op jit(solution)/shard_map/psum | solution.py:154
Sparse Core Ops, SparseCore 0:
  11.3 70.2 all-gather.4
  190.0 184.0 all-reduce.2
  411.2 157.0 all-reduce.4
Sparse Core Ops, SparseCore 1:
  192.0 50.1 all-gather.6
  244.2 41.2 all-gather.10
  287.5 50.4 all-gather.8
